TPU v7x, 32 devices: a whole 2x2x4 slice. The times are simulated.
32 devices in a mesh: dp: 4 (over z), tensor: 8 (over y, x, core).
Axes of the slice: x: 2, y: 2, z: 4, core: 2. Of those that a mesh axis runs over, the one named last changes fastest.
Arguments:
- hidden_in: bfloat16 [4, 1024, 2304], P('dp', 'tensor'), may hold values from -6 to 6
- prompt_len: int32 [4], P('dp'), may hold values from 1 to 1024, 2560 in all
- start_pos: int32 [4], P('dp'), may hold values from 0 to 511
- routes: int32 [4, 1024, 2], P('dp'), may hold values from 0 to 7, as said below
- trainer_qkv: float32 [2304, 3, 2048], P(('tensor', 'dp')), may hold values from -1 to 1
- trainer_out: float32 [2048, 2304], P(('tensor', 'dp')), may hold values from -0.125 to 0.125
- trainer_gate: float32 [2304, 5760], P('tensor'), may hold values from -0.125 to 0.125
- trainer_up: float32 [2304, 5760], P('tensor'), may hold values from -0.125 to 0.125
- trainer_down: float32 [2304, 5760], P('tensor'), may hold values from -0.078125 to 0.078125
- attn_gain: float32 [2304], replicated, may hold values from 0.25 to 1.75
- moe_gain: float32 [2304], replicated, may hold values from 0.25 to 1.75
- router: bfloat16 [2304, 8], replicated, may hold values from -0.125 to 0.125
Outputs:
- server_qkv: bfloat16 [2304, 3, 2048], P(None, None, 'tensor')
- server_out: bfloat16 [2048, 2304], P('tensor')
- server_gate: bfloat16 [2304, 5760], P(None, 'tensor')
- server_up: bfloat16 [2304, 5760], P(None, 'tensor')
- server_down: bfloat16 [2304, 5760], P(None, 'tensor')
- hidden_out: bfloat16 [4, 1024, 2304], P('dp', 'tensor')
- kv_cache: bfloat16 [4, 2, 1024, 2048], P('dp', None, None, 'tensor')
Inputs may be any that keep to these rules, and one draw needn't show every extreme that they name: `routes`: each row names two different experts; expert 0 is named by at most 512 rows of each prompt and by exactly 512 rows of some prompt.
All inputs are finite; a program needn't handle non-finite values. No bound on the sum of `prompt_len` on one device may be relied on, other than what follows from the above.
Results may differ from a plain program's by a relative error of at most 0.011.
The roundings to bfloat16 on the way count: a program that leaves them out, or rounds other values in their place, can miss the bound.
Values may be sent and summed in bfloat16 or wider, within the bound.
No kernel may reach another device: no remote copies, remote signals or barrier semaphores. Data moves between devices by JAX's collectives and lax.ppermute only.
A program may use at most 256 MiB of HBM per device.

v0:
```python
import jax
import jax.numpy as jnp
from jax import lax
from jax.sharding import PartitionSpec as P

HEAD_DIM = 64


def rms_scale(values, gain_row):
    mean_sq = jnp.mean(values * values, axis=-1, keepdims=True)
    return values * lax.rsqrt(mean_sq + 1e-05) * gain_row


def rotate(head_block, positions):
    half_dim = head_block.shape[-1] // 2
    inv_freq = jnp.power(
        10000.0, jnp.arange(half_dim, dtype=jnp.float32) * (-2.0 / head_block.shape[-1])
    )
    angles = positions.astype(jnp.float32)[:, None] * inv_freq[None, :]
    cosine = jnp.cos(angles)[:, None, :]
    sine_part = jnp.sin(angles)[:, None, :]
    first_half = head_block[..., :half_dim]
    second_half = head_block[..., half_dim:]
    return jnp.concatenate(
        [
            first_half * cosine - second_half * sine_part,
            second_half * cosine + first_half * sine_part,
        ],
        axis=-1,
    )


def attend_block(query_blk, key_blk, value_blk, row_start):
    scores = jnp.einsum(
        "qhd,khd->hqk", query_blk, key_blk, preferred_element_type=jnp.float32
    ) * query_blk.shape[-1] ** (-0.5)
    row_ids = row_start + jnp.arange(query_blk.shape[0], dtype=jnp.int32)
    col_ids = jnp.arange(key_blk.shape[0], dtype=jnp.int32)
    scores = jnp.where(row_ids[None, :, None] >= col_ids[None, None, :], scores, -1e30)
    row_max = jnp.max(scores, axis=-1, keepdims=True)
    exp_scores = jnp.exp(scores - row_max)
    attn_probs = (exp_scores / jnp.sum(exp_scores, axis=-1, keepdims=True)).astype(jnp.bfloat16)
    return jnp.einsum(
        "hqk,khd->qhd", attn_probs, value_blk, preferred_element_type=jnp.float32
    ).astype(jnp.bfloat16)


def shards(
    hidden_in,
    prompt_len,
    start_pos,
    routes,
    trainer_qkv,
    trainer_out,
    trainer_gate,
    trainer_up,
    trainer_down,
    attn_gain,
    moe_gain,
    router,
):
    tensor_size = lax.axis_size("tensor")
    replica_count = lax.axis_size("dp")
    expert_mats = (
        lax.all_to_all(
            trainer_gate.astype(jnp.bfloat16), "tensor", split_axis=1, concat_axis=0, tiled=True
        ),
        lax.all_to_all(
            trainer_up.astype(jnp.bfloat16), "tensor", split_axis=1, concat_axis=0, tiled=True
        ),
        lax.all_to_all(
            trainer_down.astype(jnp.bfloat16), "tensor", split_axis=1, concat_axis=0, tiled=True
        ),
    )
    server_gate, server_up, server_down = expert_mats
    qkv_cast = trainer_qkv.astype(jnp.bfloat16)
    out_cast = trainer_out.astype(jnp.bfloat16)
    column_part = lax.all_to_all(qkv_cast, "tensor", split_axis=2, concat_axis=0, tiled=True)
    stacked, server_out = (
        lax.all_gather(column_part, "dp", axis=0, tiled=True),
        lax.all_gather(out_cast, "dp", axis=0, tiled=True),
    )
    block_rows = stacked.shape[0] // (replica_count * tensor_size)
    server_qkv = (
        stacked.reshape(replica_count, tensor_size, block_rows, 3, stacked.shape[2])
        .transpose(1, 0, 2, 3, 4)
        .reshape(stacked.shape)
    )
    rows_dev = hidden_in.shape[1]
    seq_len = rows_dev * tensor_size
    length = prompt_len[0]
    offset = start_pos[0]
    my_first = lax.axis_index("tensor") * rows_dev
    tokens = hidden_in[0].astype(jnp.float32)
    normed = rms_scale(tokens, attn_gain).astype(jnp.bfloat16)
    local_width = server_qkv.shape[2]
    heads_here = local_width // HEAD_DIM
    piece = lax.all_gather(normed, "tensor", axis=0, tiled=True)
    mixed = jnp.einsum("sd,dtc->stc", piece, server_qkv, preferred_element_type=jnp.float32)
    places = offset + jnp.arange(piece.shape[0], dtype=jnp.int32)
    query_rot = rotate(mixed[:, 0].reshape(-1, heads_here, HEAD_DIM), places).reshape(
        -1, local_width
    )
    key_rot = rotate(mixed[:, 1].reshape(-1, heads_here, HEAD_DIM), places).reshape(-1, local_width)
    qkv_rows = jnp.stack([query_rot, key_rot, mixed[:, 2]], axis=1).astype(jnp.bfloat16)
    query_all = qkv_rows[:, 0].reshape(seq_len, heads_here, HEAD_DIM)
    keys_all = qkv_rows[:, 1].reshape(seq_len, heads_here, HEAD_DIM)
    values_all = qkv_rows[:, 2].reshape(seq_len, heads_here, HEAD_DIM)
    block_len = min(512, seq_len)
    block_outs = []
    for block_id in range(seq_len // block_len):
        row_lo = block_id * block_len
        row_hi = row_lo + block_len
        query_blk = query_all[row_lo:row_hi]
        key_blk = keys_all[:row_hi]
        value_blk = values_all[:row_hi]
        block_result = attend_block(query_blk, key_blk, value_blk, row_lo)
        block_outs.append(block_result)
    attended = jnp.concatenate(block_outs, axis=0).reshape(seq_len, local_width)
    attn_sum = lax.psum_scatter(
        jnp.dot(attended, server_out, preferred_element_type=jnp.float32).astype(jnp.bfloat16),
        "tensor",
        scatter_dimension=0,
        tiled=True,
    ).astype(jnp.float32)
    middle = (tokens + attn_sum).astype(jnp.bfloat16)
    normed_moe = rms_scale(middle.astype(jnp.float32), moe_gain).astype(jnp.bfloat16)
    local_routes = lax.dynamic_slice_in_dim(routes[0], my_first, rows_dev, 0)
    local_valid = my_first + jnp.arange(rows_dev, dtype=jnp.int32) < length
    logits = jnp.dot(normed_moe, router, preferred_element_type=jnp.float32)
    expert_ids = jnp.arange(router.shape[1], dtype=jnp.int32)
    logit_first = jnp.sum(
        jnp.where(local_routes[:, 0:1] == expert_ids[None, :], logits, 0.0), axis=1
    )
    logit_second = jnp.sum(
        jnp.where(local_routes[:, 1:2] == expert_ids[None, :], logits, 0.0), axis=1
    )
    other_logit = jnp.where(local_routes[:, 0] == 0, logit_second, logit_first)
    local_routed = jnp.any(local_routes == 0, axis=1)
    route_w = jnp.where(local_routed, jax.nn.sigmoid(logits[:, 0] - other_logit), 0.0)
    gathered = lax.all_gather(normed_moe, "tensor", axis=0, tiled=True)
    seq_ids = jnp.arange(seq_len, dtype=jnp.int32)
    all_routed = jnp.any(routes[0] == 0, axis=1)
    capacity = seq_len // 2
    slot = jnp.cumsum(all_routed.astype(jnp.int32)) - 1
    slot_rows = (
        jnp.full((capacity,), seq_len, jnp.int32)
        .at[jnp.where(all_routed, slot, capacity)]
        .set(seq_ids, mode="drop")
    )
    picked = gathered[jnp.minimum(slot_rows, seq_len - 1)]
    gate_val = jnp.dot(picked, server_gate, preferred_element_type=jnp.float32)
    up_val = jnp.dot(picked, server_up, preferred_element_type=jnp.float32)
    act = (jax.nn.silu(gate_val) * up_val).astype(jnp.bfloat16)
    slot_sums = lax.dot_general(
        act, server_down, (((1,), (1,)), ((), ())), preferred_element_type=jnp.float32
    )
    terms = (
        jnp.zeros((seq_len, normed_moe.shape[1]), jnp.float32)
        .at[slot_rows]
        .add(slot_sums, mode="drop")
    )
    expert_sum = lax.psum_scatter(
        terms.astype(jnp.bfloat16), "tensor", scatter_dimension=0, tiled=True
    ).astype(jnp.float32)
    result = middle.astype(jnp.float32) + route_w[:, None] * expert_sum
    hidden_out = jnp.where(local_valid[:, None], result, 0.0).astype(jnp.bfloat16)[None]
    seq_valid = jnp.arange(seq_len, dtype=jnp.int32) < length
    cache_pair = jnp.where(
        seq_valid[None, :, None], qkv_rows[:, 1:3].transpose(1, 0, 2), jnp.zeros((), jnp.bfloat16)
    )
    return (
        server_qkv,
        server_out,
        server_gate,
        server_up,
        server_down,
        hidden_out,
        cache_pair[None],
    )


def solution(mesh):
    placed = (
        P("dp", "tensor", None),
        P("dp"),
        P("dp"),
        P("dp", None, None),
        P(("tensor", "dp"), None, None),
        P(("tensor", "dp"), None),
        P("tensor", None),
        P("tensor", None),
        P("tensor", None),
        P(),
        P(),
        P(),
    )
    return jax.shard_map(
        shards,
        mesh=mesh,
        in_specs=placed,
        out_specs=(
            P(None, None, "tensor"),
            P("tensor", None),
            P(None, "tensor"),
            P(None, "tensor"),
            P(None, "tensor"),
            P("dp", "tensor", None),
            P("dp", None, None, "tensor"),
        ),
        check_vma=False,
    )
```

profile of v0, /device:TPU:0, one launch (start us, length us, event | category | flops | bytes accessed | tf_op | source)
XLA Modules:
  0.0 508.5 jit_solution(11771919291552511364)
XLA Ops:
  7.2 2.5 convert_element_type.86
  9.7 2.9 copy.59
  12.6 3.7 reshape.272
  16.3 18.9 %all_to_all.75 = bf16[8,2,27648]{2,1,0:T(2,128)(2,1)} all-to-all(bf16[8,2,27648]{2,1,0:T(2,128)(2,1)} %reshape.272), channel_id=1, replica_groups=mesh['dp'=4,'tensor'=8] {'tensor'}, dimensions={0} | all-to-all | bytes 1769472 | tf_op jit(solution)/shard_map/all_to_all | solution.py:78
  35.2 4.5 reshape.273
  39.7 2.2 copy.75
  42.0 0.2 fusion.23
  42.2 1.0 fusion.25
  43.3 0.7 convert_element_type.87
  44.1 0.3 reduce-scatter.3.cloned.1.call-start
  44.4 0.1 iota_compare_fusion.1
  45.2 0.4 iota_compare_fusion
  45.5 0.5 multiply_cosine_fusion
  46.1 65.7 %all-gather.5.cloned.1.call-done = bf16[2304,3,256]{2,0,1:T(8,128)(2,1)} async-done(((bf16[576,3,256]{2,0,1:T(8,128)(2,1)}), bf16[2304,3,256]{2,0,1:T(8,128)(2,1)}) %all-gather.5.cloned.1.call-update) | async-done | bytes 3538960 | tf_op jit(solution)/shard_map/all_gather | solution.py:80
  111.8 4.2 copy.62
  115.9 35.8 %all-gather.9.cloned.1.call-done = bf16[1024,2304]{1,0:T(8,128)(2,1)} async-done(((bf16[128,2304]{1,0:T(8,128)(2,1)}), bf16[1024,2304]{1,0:T(8,128)(2,1)}) %all-gather.9.cloned.1.call-update) | async-done | bytes 4718608 | tf_op jit(solution)/shard_map/all_gather | solution.py:98
  151.8 6.8 %fusion.61 = (bf16[1024,3,256]{0,2,1:T(8,128)(2,1)S(1)}, f32[1024,3,256]{0,2,1:T(8,128)S(1)}) fusion(bf16[2304,3,256]{2,0,1:T(8,128)(2,1)} %bitcast.102, bf16[1024,2304]{1,0:T(8,128)(2,1)} %all-gather.9.cloned.1.call-done), kind=kOutput, calls=%fused_computation.108 | convolution fusion | flops 3624665088 | bytes 12976128 | tf_op jit(solution)/shard_map/sd,dtc->stc/dot_general | solution.py:99
  158.7 0.1 fusion.60
  158.8 0.3 subtract_convert_fusion
  159.2 5.4 %fusion.62 = (f32[4,512]{1,0:T(4,128)S(1)}, f32[4,512,1024]{2,1,0:T(8,128)}) fusion(pred[512,1024]{1,0:T(8,128)(4,1)S(1)} %iota_compare_fusion, bf16[1024,4,32]{0,2,1:T(8,128)(2,1)S(1)} %get-tuple-element.52, bf16[1024,4,32]{0,2,1:T(8,128)(2,1)S(1)} %get-tuple-element.53, bf16[1024,4,32]{0,2,1:T(8,128)(2,1)S(1)} %get-tuple-element.49, ...), kind=kOutput, calls=%fused_computation.109 | convolution fusion | flops 278397952 | bytes 9969664 | tf_op jit(solution)/shard_map/sub | solution.py:41
  164.6 3.7 fusion.63
  168.2 2.9 fusion.28
  171.1 1.8 copy-done.13
  172.9 1.5 fusion.27
  174.5 10.0 %all-gather.7.cloned.1.call-done = bf16[256,2304]{1,0:T(8,128)(2,1)} async-done(((bf16[64,2304]{1,0:T(8,128)(2,1)}), bf16[256,2304]{1,0:T(8,128)(2,1)}) %all-gather.7.cloned.1.call-update) | async-done | bytes 1179664 | tf_op jit(solution)/shard_map/all_gather | solution.py:81
  184.4 4.8 convolution_convert_fusion
  189.3 0.6 all-gather.11.cloned.1.call-start
  189.9 52.6 %reduce-scatter.3.cloned.1.call-done = bf16[128,2304]{1,0:T(8,128)(2,1)} async-done(((bf16[1024,2304]{1,0:T(8,128)(2,1)}), bf16[128,2304]{1,0:T(8,128)(2,1)}) %reduce-scatter.3.cloned.1.call-update) | async-done | bytes 589840 | tf_op jit(solution)/shard_map/reduce_scatter | solution.py:120
  242.4 1.3 fusion.18
  243.8 2.1 fusion.20
  246.0 4.9 convert_element_type.88
  250.9 8.5 %all_to_all.59 = bf16[288,8,720]{2,1,0:T(8,128)(2,1)} reshape(bf16[288,5760]{1,0:T(8,128)(2,1)} %convert_element_type.88) | data formatting | bytes 6635520 | tf_op jit(solution)/shard_map/all_to_all | solution.py:65
  259.4 4.6 copy.63
  264.0 4.5 all-to-all-start.1
  268.4 5.0 convert_element_type.89
  273.4 8.5 %all_to_all.63 = bf16[288,8,720]{2,1,0:T(8,128)(2,1)} reshape(bf16[288,5760]{1,0:T(8,128)(2,1)} %convert_element_type.89) | data formatting | bytes 6635520 | tf_op jit(solution)/shard_map/all_to_all | solution.py:68
  281.9 4.4 copy.64
  286.4 35.8 %all-to-all-done.1 = bf16[288,8,720]{2,0,1:T(8,128)(2,1)} async-done(((bf16[288,8,720]{2,0,1:T(8,128)(2,1)}), bf16[288,8,720]{2,0,1:T(8,128)(2,1)}, u32[]{:S(2)}, u32[]{:S(2)}) %all-to-all-start.1) | async-done | bytes 3317792 | tf_op jit(solution)/shard_map/all_to_all | solution.py:65
  322.2 4.5 all-to-all-start.2
  326.7 4.9 convert_element_type.90
  331.6 8.4 %all_to_all.67 = bf16[288,8,720]{2,1,0:T(8,128)(2,1)} reshape(bf16[288,5760]{1,0:T(8,128)(2,1)} %convert_element_type.90) | data formatting | bytes 6635520 | tf_op jit(solution)/shard_map/all_to_all | solution.py:71
  340.1 4.6 copy.65
  344.6 24.2 %all-to-all-done.2 = bf16[288,8,720]{2,0,1:T(8,128)(2,1)} async-done(((bf16[288,8,720]{2,0,1:T(8,128)(2,1)}), bf16[288,8,720]{2,0,1:T(8,128)(2,1)}, u32[]{:S(2)}, u32[]{:S(2)}) %all-to-all-start.2) | async-done | bytes 3317792 | tf_op jit(solution)/shard_map/all_to_all | solution.py:68
  368.8 4.5 all-to-all-start.3
  373.4 0.3 reduce-window.9
  373.7 0.1 slice.89
  373.8 0.1 slice_reduce_fusion
  373.9 0.1 add_add_fusion
  374.0 4.5 scatter_custom_fusion
  378.5 7.8 %gather_fusion = bf16[512,2304]{1,0:T(8,128)(2,1)S(1)} fusion(bf16[1024,2304]{1,0:T(8,128)(2,1)} %all-gather.11.cloned.1.call-done, s32[1024]{0:T(1024)S(1)} %pad_clamp_fusion), kind=kCustom, calls=%fused_computation | custom fusion | bytes 4720640 | tf_op jit(solution)/shard_map/gather | solution.py:151
  386.4 5.0 fusion.72
  391.4 24.0 %all-to-all-done.3 = bf16[288,8,720]{2,0,1:T(8,128)(2,1)} async-done(((bf16[288,8,720]{2,0,1:T(8,128)(2,1)}), bf16[288,8,720]{2,0,1:T(8,128)(2,1)}, u32[]{:S(2)}, u32[]{:S(2)}) %all-to-all-start.3) | async-done | bytes 3317792 | tf_op jit(solution)/shard_map/all_to_all | solution.py:71
  415.4 9.9 %fusion.32 = f32[512,2304]{1,0:T(8,128)} fusion(bf16[2304,720]{1,0:T(8,128)(2,1)} %bitcast.12, f32[512,720]{0,1:T(8,128)} %fusion.72, bf16[512,2304]{1,0:T(8,128)(2,1)S(1)} %gather_fusion, bf16[2304,720]{1,0:T(8,128)(2,1)} %bitcast.10), kind=kOutput, calls=%fused_computation.51 | convolution fusion | flops 3399598080 | bytes 15187968 | tf_op jit(solution)/shard_map/dot_general | solution.py:155
  425.3 13.3 %scatter_custom_fusion.1 = f32[1024,2304]{1,0:T(8,128)} fusion(s32[512]{0:T(512)S(1)} %get-tuple-element.57, f32[512,2304]{1,0:T(8,128)} %fusion.32, f32[]{:T(128)} %constant.20.clone.1), kind=kCustom, calls=%fused_computation.12 | custom fusion | flops 1179648 | bytes 9437696 | tf_op jit(solution)/shard_map/scatter-add | solution.py:161
  438.6 6.4 %convert_element_type.109 = bf16[1024,2304]{1,0:T(8,128)(2,1)} convert(f32[1024,2304]{1,0:T(8,128)} %scatter_custom_fusion.1) | non-fusion elementwise | flops 2359296 | bytes 14155776 | tf_op jit(solution)/shard_map/convert_element_type | solution.py:164
  445.7 5.7 %copy.68 = bf16[2304,720]{0,1:T(8,128)(2,1)} copy(bf16[2304,720]{1,0:T(8,128)(2,1)} %bitcast.8) | data formatting | bytes 6635520
  451.4 5.9 %copy.69 = bf16[2304,720]{0,1:T(8,128)(2,1)} copy(bf16[2304,720]{1,0:T(8,128)(2,1)} %bitcast.10) | data formatting | bytes 6635520
  457.3 5.7 %copy.70 = bf16[2304,720]{0,1:T(8,128)(2,1)} copy(bf16[2304,720]{1,0:T(8,128)(2,1)} %bitcast.12) | data formatting | bytes 6635520
  463.2 1.1 fusion.29
  464.2 2.3 copy.71
  466.5 0.2 select_reduce_fusion.1
  466.8 31.4 %reduce-scatter.5.cloned.1.call-done = bf16[128,2304]{1,0:T(8,128)(2,1)} async-done(((bf16[1024,2304]{1,0:T(8,128)(2,1)}), bf16[128,2304]{1,0:T(8,128)(2,1)}) %reduce-scatter.5.cloned.1.call-update) | async-done | bytes 589840 | tf_op jit(solution)/shard_map/reduce_scatter | solution.py:163
  498.2 2.2 fusion.33
  500.4 1.0 copy.79
  (59 shorter events, 0.7 us)
Async XLA Ops:
  7.2 459.3 %copy-start = (bf16[2304,8]{0,1:T(8,128)(2,1)S(1)}, bf16[2304,8]{0,1:T(8,128)(2,1)}, u32[]{:S(2)}) copy-start(bf16[2304,8]{0,1:T(8,128)(2,1)} %param.23) | copy-start | bytes 110596
  7.2 104.6 %all-gather.5.cloned.1.call-start = ((), (), s32[]{:S(2)}) async-start(), calls=%async_computation.6 | async-start | bytes 4423680 | tf_op jit(solution)/shard_map/all_gather | solution.py:80
  35.2 6.8 %copy-start.1 = (bf16[1,128,2304]{2,1,0:T(8,128)(2,1)S(1)}, bf16[1,128,2304]{2,1,0:T(8,128)(2,1)}, u32[]{:S(2)}) copy-start(bf16[1,128,2304]{2,1,0:T(8,128)(2,1)} %param.12) | copy-start | bytes 1769476
  35.2 7.0 %copy-start.10 = (f32[2304]{0:T(1024)S(1)}, f32[2304]{0:T(1024)}, u32[]{:S(2)}) copy-start(f32[2304]{0:T(1024)} %param.21) | copy-start | bytes 27652
  39.7 3.6 copy-start.9
  41.9 109.9 %all-gather.9.cloned.1.call-start = ((), (), s32[]{:S(2)}) async-start(), calls=%async_computation.8 | async-start | bytes 5308416 | tf_op jit(solution)/shard_map/all_gather | solution.py:98
  43.2 141.2 %all-gather.7.cloned.1.call-start = ((), (), s32[]{:S(2)}) async-start(), calls=%async_computation.7 | async-start | bytes 1474560 | tf_op jit(solution)/shard_map/all_gather | solution.py:81
  44.1 198.4 %reduce-scatter.3.cloned.1.call-start = ((), (), s32[]{:S(2)}) async-start(), calls=%async_computation.9 | async-start | bytes 5308416 | tf_op jit(solution)/shard_map/reduce_scatter | solution.py:120
  159.2 5.4 %copy-start.5 = (bf16[1024,4,32]{0,2,1:T(8,128)(2,1)}, bf16[1024,4,32]{0,2,1:T(8,128)(2,1)S(1)}, u32[]{:S(2)}) copy-start(bf16[1024,4,32]{0,2,1:T(8,128)(2,1)S(1)} %get-tuple-element.48) | copy-start | bytes 786436
  159.2 5.4 %copy-start.7 = (bf16[1024,4,32]{0,2,1:T(8,128)(2,1)}, bf16[1024,4,32]{0,2,1:T(8,128)(2,1)S(1)}, u32[]{:S(2)}) copy-start(bf16[1024,4,32]{0,2,1:T(8,128)(2,1)S(1)} %get-tuple-element.49) | copy-start | bytes 786436
  168.2 4.7 copy-start.13
  189.3 54.5 %copy-start.11 = (f32[2304]{0:T(1024)S(1)}, f32[2304]{0:T(1024)}, u32[]{:S(2)}) copy-start(f32[2304]{0:T(1024)} %param.22) | copy-start | bytes 27652
  189.3 189.2 %all-gather.11.cloned.1.call-start = ((), (), s32[]{:S(2)}) async-start(), calls=%async_computation.10 | async-start | bytes 5308416 | tf_op jit(solution)/shard_map/all_gather | solution.py:141
  264.0 58.2 %all-to-all-start.1 = ((bf16[288,8,720]{2,0,1:T(8,128)(2,1)}), bf16[288,8,720]{2,0,1:T(8,128)(2,1)}, u32[]{:S(2)}, u32[]{:S(2)}) async-start(bf16[288,8,720]{2,0,1:T(8,128)(2,1)} %copy.63), calls=%async_computation.1 | async-start | bytes 7077888 | tf_op jit(solution)/shard_map/all_to_all | solution.py:65
  322.2 46.6 %all-to-all-start.2 = ((bf16[288,8,720]{2,0,1:T(8,128)(2,1)}), bf16[288,8,720]{2,0,1:T(8,128)(2,1)}, u32[]{:S(2)}, u32[]{:S(2)}) async-start(bf16[288,8,720]{2,0,1:T(8,128)(2,1)} %copy.64), calls=%async_computation.2 | async-start | bytes 7077888 | tf_op jit(solution)/shard_map/all_to_all | solution.py:68
  344.6 28.7 %copy-start.12 = (s32[1,1024,2]{1,2,0:T(2,128)S(1)}, s32[1,1024,2]{1,2,0:T(2,128)}, u32[]{:S(2)}) copy-start(s32[1,1024,2]{1,2,0:T(2,128)} %param.15) | copy-start | bytes 24580
  368.8 46.6 %all-to-all-start.3 = ((bf16[288,8,720]{2,0,1:T(8,128)(2,1)}), bf16[288,8,720]{2,0,1:T(8,128)(2,1)}, u32[]{:S(2)}, u32[]{:S(2)}) async-start(bf16[288,8,720]{2,0,1:T(8,128)(2,1)} %copy.65), calls=%async_computation.3 | async-start | bytes 7077888 | tf_op jit(solution)/shard_map/all_to_all | solution.py:71
  373.3 124.9 %reduce-scatter.5.cloned.1.call-start = ((), (), s32[]{:S(2)}) async-start(), calls=%async_computation.11 | async-start | bytes 5308416 | tf_op jit(solution)/shard_map/reduce_scatter | solution.py:163
  457.3 5.7 %copy-start.6 = (bf16[1024,4,32]{0,2,1:T(8,128)(2,1)S(1)}, bf16[1024,4,32]{0,2,1:T(8,128)(2,1)}, u32[]{:S(2)}) copy-start(bf16[1024,4,32]{0,2,1:T(8,128)(2,1)} %copy-done.5) | copy-start | bytes 786436
  457.3 5.7 %copy-start.8 = (bf16[1024,4,32]{0,2,1:T(8,128)(2,1)S(1)}, bf16[1024,4,32]{0,2,1:T(8,128)(2,1)}, u32[]{:S(2)}) copy-start(bf16[1024,4,32]{0,2,1:T(8,128)(2,1)} %copy-done.7) | copy-start | bytes 786436
  463.1 3.4 copy-start.2
  463.1 35.1 %copy-start.3 = (bf16[128,2304]{1,0:T(8,128)(2,1)S(1)}, bf16[128,2304]{1,0:T(8,128)(2,1)}, u32[]{:S(2)}) copy-start(bf16[128,2304]{1,0:T(8,128)(2,1)} %reduce-scatter.3.cloned.1.call-done) | copy-start | bytes 1769476
  463.1 37.3 %copy-start.4 = (bf16[256,2304]{1,0:T(8,128)(2,1)S(1)}, bf16[256,2304]{1,0:T(8,128)(2,1)}, u32[]{:S(2)}) copy-start(bf16[256,2304]{1,0:T(8,128)(2,1)} %all-gather.7.cloned.1.call-done) | copy-start | bytes 3538948
Sparse Core Ops, SparseCore 0:
  42.0 69.6 all-gather.4
  114.2 37.5 all-gather.8
  153.9 30.4 all-gather.6
  189.4 52.9 reduce-scatter.2
  246.1 60.3 all-gather.10
  445.1 53.0 reduce-scatter.4
where the time goes:
time: 513 us; the launch traced here: 509 us
  waiting for transfers between devices  279 us (54%)
  local copies, waits for them, and re-layouts  91.6 us (18%)
  other arithmetic  47.8 us (9%)
  matrix products  40.3 us (8%)
  blocking collectives  18.9 us (4%)
  between operations  16 us (3%)
  starting transfers between devices  14.5 us (3%)
    all_gather x1, waiting for transfers between devices, shards(): lax.all_gather(column_part, 'dp', axis=0, tiled=True)  65.7 us
    reduce_scatter x1, waiting for transfers between devices, shards(): lax.psum_scatter(jnp.dot(attended, server_out, preferred_element_type=jnp...  52.6 us
    all_gather x1, waiting for transfers between devices, shards(): piece = lax.all_gather(normed, 'tensor', axis=0, tiled=True)  35.8 us
    all_to_all x1, waiting for transfers between devices, shards(): lax.all_to_all(trainer_gate.astype(jnp.bfloat16), 'tensor', split_axis=1,...  35.8 us
    reduce_scatter x1, waiting for transfers between devices, shards(): lax.psum_scatter(terms.astype(jnp.bfloat16), 'tensor', scatter_dimension=...  31.4 us
    unnamed x35, local copies, waits for them, and re-layouts  30.7 us
    all_to_all x1, waiting for transfers between devices, shards(): lax.all_to_all(trainer_up.astype(jnp.bfloat16), 'tensor', split_axis=1, c...  24.2 us
    all_to_all x1, waiting for transfers between devices, shards(): lax.all_to_all(trainer_down.astype(jnp.bfloat16), 'tensor', split_axis=1,...  24 us
  transfers between devices with their start and end apart: 9, of which 8 were waited for; matrix products, arithmetic and copies ran while one was open for 19% of the time, Pallas kernels for 0%

commit v1 on v0

--- a/solution.py
+++ b/solution.py
@@ -95,7 +95,14 @@
     normed = rms_scale(tokens, attn_gain).astype(jnp.bfloat16)
     local_width = server_qkv.shape[2]
     heads_here = local_width // HEAD_DIM
-    piece = lax.all_gather(normed, "tensor", axis=0, tiled=True)
+    ring = [normed]
+    for hop in range(7):
+        ring.append(lax.ppermute(ring[-1], "tensor", [(dev, (dev + 1) % 8) for dev in range(8)]))
+    piece = jnp.roll(
+        jnp.concatenate(ring[::-1], axis=0),
+        (lax.axis_index("tensor") + 1) * ring[0].shape[0],
+        axis=0,
+    )
     mixed = jnp.einsum("sd,dtc->stc", piece, server_qkv, preferred_element_type=jnp.float32)
     places = offset + jnp.arange(piece.shape[0], dtype=jnp.int32)
     query_rot = rotate(mixed[:, 0].reshape(-1, heads_here, HEAD_DIM), places).reshape(

time: 513 us -> 492 us (0.959)
  waiting for transfers between devices: 279 us -> 235 us
  local copies, waits for them, and re-layouts: 91.6 us -> 110 us
    ppermute x0 -> x7, waiting for transfers between devices: none -> 66.4 us  [shards(): lax.ppermute(ring[-1], 'tensor', [(dev, (dev + 1) % 8) for dev in range(8)])]
    all_gather x1, waiting for transfers between devices: 65.7 us -> 0.01 us  [shards(): lax.all_gather(column_part, 'dp', axis=0, tiled=True)]
    all_gather x1 -> x0, waiting for transfers between devices: 35.8 us -> none  [shards(): piece = lax.all_gather(normed, 'tensor', axis=0, tiled=True)]
    unnamed x35 -> x59, local copies, waits for them, and re-layouts: 30.7 us -> 49.7 us
    all_gather x1, waiting for transfers between devices: 9.96 us -> 0.02 us  [shards(): lax.all_gather(out_cast, 'dp', axis=0, tiled=True)]
  transfers between devices with their start and end apart: 9 -> 15, of which waited for: 8 -> 12; matrix products, arithmetic and copies ran while one was open for 19% -> 24% of each run, Pallas kernels for 0% -> 0%
where the time goes in v1:
time: 492 us; the launch traced here: 487 us
  waiting for transfers between devices  235 us (48%)
  local copies, waits for them, and re-layouts  110 us (22%)
  other arithmetic  52.3 us (11%)
  matrix products  40.5 us (8%)
  blocking collectives  18.9 us (4%)
  between operations  15.7 us (3%)
  starting transfers between devices  14.5 us (3%)
    ppermute x7, waiting for transfers between devices, shards(): lax.ppermute(ring[-1], 'tensor', [(dev, (dev + 1) % 8) for dev in range(8)])  66.4 us
    reduce_scatter x1, waiting for transfers between devices, shards(): lax.psum_scatter(jnp.dot(attended, server_out, preferred_element_type=jnp...  53.2 us
    unnamed x59, local copies, waits for them, and re-layouts  49.7 us
    all_to_all x1, waiting for transfers between devices, shards(): lax.all_to_all(trainer_gate.astype(jnp.bfloat16), 'tensor', split_axis=1,...  35.8 us
    reduce_scatter x1, waiting for transfers between devices, shards(): lax.psum_scatter(terms.astype(jnp.bfloat16), 'tensor', scatter_dimension=...  31.4 us
    all_to_all x1, waiting for transfers between devices, shards(): lax.all_to_all(trainer_up.astype(jnp.bfloat16), 'tensor', split_axis=1, c...  24.2 us
    all_to_all x1, waiting for transfers between devices, shards(): lax.all_to_all(trainer_down.astype(jnp.bfloat16), 'tensor', split_axis=1,...  24 us
    all_to_all x1, blocking collectives, shards(): lax.all_to_all(qkv_cast, 'tensor', split_axis=2, concat_axis=0, tiled=True)  18.9 us
  transfers between devices with their start and end apart: 15, of which 12 were waited for; matrix products, arithmetic and copies ran while one was open for 24% of the time, Pallas kernels for 0%

profile of v1, /device:TPU:0, one launch (start us, length us, event | category | flops | bytes accessed | tf_op | source)
XLA Modules:
  0.0 486.5 jit_solution(11267279683598034004)
XLA Ops:
  7.2 2.5 convert_element_type.86
  9.7 2.9 copy.59
  12.6 3.7 reshape.272
  16.3 18.9 %all_to_all.75 = bf16[8,2,27648]{2,1,0:T(2,128)(2,1)} all-to-all(bf16[8,2,27648]{2,1,0:T(2,128)(2,1)} %reshape.272), channel_id=1, replica_groups=mesh['dp'=4,'tensor'=8] {'tensor'}, dimensions={0} | all-to-all | bytes 1769472 | tf_op jit(solution)/shard_map/all_to_all | solution.py:78
  35.2 4.5 reshape.273
  39.7 2.2 copy.75
  42.5 10.2 %collective-permute-done = bf16[128,2304]{1,0:T(8,128)(2,1)S(1)} collective-permute-done((bf16[128,2304]{1,0:T(8,128)(2,1)S(1)}, bf16[128,2304]{1,0:T(8,128)(2,1)S(1)}, u32[]{:S(2)}, u32[]{:S(2)}) %collective-permute-start) | collective-permute-done | bytes 589856 | tf_op jit(solution)/shard_map/ppermute | solution.py:100
  52.7 10.2 %collective-permute-done.1 = bf16[128,2304]{1,0:T(8,128)(2,1)S(1)} collective-permute-done((bf16[128,2304]{1,0:T(8,128)(2,1)S(1)}, bf16[128,2304]{1,0:T(8,128)(2,1)S(1)}, u32[]{:S(2)}, u32[]{:S(2)}) %collective-permute-start.1) | collective-permute-done | bytes 589856 | tf_op jit(solution)/shard_map/ppermute | solution.py:100
  62.9 10.2 %collective-permute-done.2 = bf16[128,2304]{1,0:T(8,128)(2,1)S(1)} collective-permute-done((bf16[128,2304]{1,0:T(8,128)(2,1)S(1)}, bf16[128,2304]{1,0:T(8,128)(2,1)S(1)}, u32[]{:S(2)}, u32[]{:S(2)}) %collective-permute-start.2) | collective-permute-done | bytes 589856 | tf_op jit(solution)/shard_map/ppermute | solution.py:100
  73.1 10.2 %collective-permute-done.3 = bf16[128,2304]{1,0:T(8,128)(2,1)S(1)} collective-permute-done((bf16[128,2304]{1,0:T(8,128)(2,1)S(1)}, bf16[128,2304]{1,0:T(8,128)(2,1)S(1)}, u32[]{:S(2)}, u32[]{:S(2)}) %collective-permute-start.3) | collective-permute-done | bytes 589856 | tf_op jit(solution)/shard_map/ppermute | solution.py:100
  83.3 10.3 %collective-permute-done.4 = bf16[128,2304]{1,0:T(8,128)(2,1)} collective-permute-done((bf16[128,2304]{1,0:T(8,128)(2,1)S(1)}, bf16[128,2304]{1,0:T(8,128)(2,1)}, u32[]{:S(2)}, u32[]{:S(2)}) %collective-permute-start.4) | collective-permute-done | bytes 589856 | tf_op jit(solution)/shard_map/ppermute | solution.py:100
  93.6 1.8 convert_element_type.87
  96.1 8.0 %collective-permute-done.5 = bf16[128,2304]{1,0:T(8,128)(2,1)} collective-permute-done((bf16[128,2304]{1,0:T(8,128)(2,1)}, bf16[128,2304]{1,0:T(8,128)(2,1)}, u32[]{:S(2)}, u32[]{:S(2)}) %collective-permute-start.5) | collective-permute-done | bytes 589856 | tf_op jit(solution)/shard_map/ppermute | solution.py:100
  105.2 1.2 multiply_cosine_fusion
  106.4 1.2 iota_compare_fusion
  107.6 7.3 %collective-permute-done.6 = bf16[128,2304]{1,0:T(8,128)(2,1)} collective-permute-done((bf16[128,2304]{1,0:T(8,128)(2,1)}, bf16[128,2304]{1,0:T(8,128)(2,1)}, u32[]{:S(2)}, u32[]{:S(2)}) %collective-permute-start.6) | collective-permute-done | bytes 589856 | tf_op jit(solution)/shard_map/ppermute | solution.py:100
  114.9 1.9 constant_dynamic-update-slice_fusion.15
  116.8 1.9 constant_dynamic-update-slice_fusion.14
  118.7 2.0 constant_dynamic-update-slice_fusion.13
  124.1 1.0 constant_dynamic-update-slice_fusion.8
  125.2 1.9 constant_dynamic-update-slice_fusion.7
  127.1 1.9 constant_dynamic-update-slice_fusion.6
  129.0 1.9 constant_dynamic-update-slice_fusion.5
  134.5 1.1 constant_dynamic-update-slice_fusion
  135.5 2.4 copy.62
  138.0 7.1 %fusion.63 = (bf16[1024,3,256]{0,2,1:T(8,128)(2,1)S(1)}, f32[1024,3,256]{0,2,1:T(8,128)S(1)}) fusion(bf16[2304,3,256]{2,0,1:T(8,128)(2,1)S(1)} %bitcast.106, bf16[2048,2304]{1,0:T(8,128)(2,1)} %constant_dynamic-update-slice_fusion, s32[]{:T(128)S(6)} %select_n.80), kind=kOutput, calls=%fused_computation.126 | convolution fusion | flops 3624665088 | bytes 12976132 | tf_op jit(solution)/shard_map/sd,dtc->stc/dot_general | solution.py:106
  146.8 3.7 fusion.65
  150.5 5.4 %fusion.64 = (f32[4,512]{1,0:T(4,128)S(1)}, f32[4,512,1024]{2,1,0:T(8,128)}) fusion(pred[512,1024]{1,0:T(8,128)(4,1)S(1)} %copy-done.10, bf16[1024,4,32]{0,2,1:T(8,128)(2,1)S(1)} %get-tuple-element.52, bf16[1024,4,32]{0,2,1:T(8,128)(2,1)S(1)} %get-tuple-element.53, bf16[1024,4,32]{0,2,1:T(8,128)(2,1)S(1)} %get-tuple-element.49, ...), kind=kOutput, calls=%fused_computation.127 | convolution fusion | flops 278397952 | bytes 9969664 | tf_op jit(solution)/shard_map/sub | solution.py:41
  155.9 2.8 fusion.29
  158.7 1.8 copy-done.18
  160.5 1.5 fusion.28
  162.1 4.9 convolution_convert_fusion
  167.5 53.2 %reduce-scatter.3.cloned.1.call-done = bf16[128,2304]{1,0:T(8,128)(2,1)} async-done(((bf16[1024,2304]{1,0:T(8,128)(2,1)}), bf16[128,2304]{1,0:T(8,128)(2,1)}) %reduce-scatter.3.cloned.1.call-update) | async-done | bytes 589840 | tf_op jit(solution)/shard_map/reduce_scatter | solution.py:127
  220.8 1.3 fusion.19
  222.1 2.1 fusion.21
  224.3 4.9 %convert_element_type.88 = bf16[288,5760]{1,0:T(8,128)(2,1)} convert(f32[288,5760]{1,0:T(8,128)} %param.18) | non-fusion elementwise | flops 1658880 | bytes 9953280 | tf_op jit(solution)/shard_map/convert_element_type | solution.py:66
  229.2 8.5 %all_to_all.59 = bf16[288,8,720]{2,1,0:T(8,128)(2,1)} reshape(bf16[288,5760]{1,0:T(8,128)(2,1)} %convert_element_type.88) | data formatting | bytes 6635520 | tf_op jit(solution)/shard_map/all_to_all | solution.py:65
  237.8 4.5 copy.63
  242.3 4.5 all-to-all-start.1
  246.8 5.0 %convert_element_type.89 = bf16[288,5760]{1,0:T(8,128)(2,1)} convert(f32[288,5760]{1,0:T(8,128)} %param.19) | non-fusion elementwise | flops 1658880 | bytes 9953280 | tf_op jit(solution)/shard_map/convert_element_type | solution.py:69
  251.8 8.5 %all_to_all.63 = bf16[288,8,720]{2,1,0:T(8,128)(2,1)} reshape(bf16[288,5760]{1,0:T(8,128)(2,1)} %convert_element_type.89) | data formatting | bytes 6635520 | tf_op jit(solution)/shard_map/all_to_all | solution.py:68
  260.3 4.5 copy.64
  264.7 35.8 %all-to-all-done.1 = bf16[288,8,720]{2,0,1:T(8,128)(2,1)} async-done(((bf16[288,8,720]{2,0,1:T(8,128)(2,1)}), bf16[288,8,720]{2,0,1:T(8,128)(2,1)}, u32[]{:S(2)}, u32[]{:S(2)}) %all-to-all-start.1) | async-done | bytes 3317792 | tf_op jit(solution)/shard_map/all_to_all | solution.py:65
  300.5 4.5 all-to-all-start.2
  305.0 4.9 %convert_element_type.90 = bf16[288,5760]{1,0:T(8,128)(2,1)} convert(f32[288,5760]{1,0:T(8,128)} %param.20) | non-fusion elementwise | flops 1658880 | bytes 9953280 | tf_op jit(solution)/shard_map/convert_element_type | solution.py:72
  310.0 8.5 %all_to_all.67 = bf16[288,8,720]{2,1,0:T(8,128)(2,1)} reshape(bf16[288,5760]{1,0:T(8,128)(2,1)} %convert_element_type.90) | data formatting | bytes 6635520 | tf_op jit(solution)/shard_map/all_to_all | solution.py:71
  318.4 4.5 copy.65
  323.0 24.2 %all-to-all-done.2 = bf16[288,8,720]{2,0,1:T(8,128)(2,1)} async-done(((bf16[288,8,720]{2,0,1:T(8,128)(2,1)}), bf16[288,8,720]{2,0,1:T(8,128)(2,1)}, u32[]{:S(2)}, u32[]{:S(2)}) %all-to-all-start.2) | async-done | bytes 3317792 | tf_op jit(solution)/shard_map/all_to_all | solution.py:68
  347.1 4.5 all-to-all-start.3
  352.3 4.5 scatter_custom_fusion
  356.9 7.8 %gather_fusion = bf16[512,2304]{1,0:T(8,128)(2,1)S(1)} fusion(bf16[1024,2304]{1,0:T(8,128)(2,1)} %all-gather.8.cloned.1.call-done, s32[1024]{0:T(1024)S(1)} %pad_clamp_fusion), kind=kCustom, calls=%fused_computation | custom fusion | bytes 4720640 | tf_op jit(solution)/shard_map/gather | solution.py:158
  364.7 5.0 %fusion.74 = f32[512,720]{0,1:T(8,128)} fusion(bf16[512,2304]{1,0:T(8,128)(2,1)S(1)} %gather_fusion, bf16[2304,720]{1,0:T(8,128)(2,1)} %bitcast.8), kind=kOutput, calls=%fused_computation.129 | convolution fusion | flops 1698693120 | bytes 7151616 | tf_op jit(solution)/shard_map/dot_general | solution.py:159
  369.8 24.0 %all-to-all-done.3 = bf16[288,8,720]{2,0,1:T(8,128)(2,1)} async-done(((bf16[288,8,720]{2,0,1:T(8,128)(2,1)}), bf16[288,8,720]{2,0,1:T(8,128)(2,1)}, u32[]{:S(2)}, u32[]{:S(2)}) %all-to-all-start.3) | async-done | bytes 3317792 | tf_op jit(solution)/shard_map/all_to_all | solution.py:71
  393.7 9.9 %fusion.33 = f32[512,2304]{1,0:T(8,128)} fusion(bf16[2304,720]{1,0:T(8,128)(2,1)} %bitcast.12, f32[512,720]{0,1:T(8,128)} %fusion.74, bf16[512,2304]{1,0:T(8,128)(2,1)S(1)} %gather_fusion, bf16[2304,720]{1,0:T(8,128)(2,1)} %bitcast.10), kind=kOutput, calls=%fused_computation.52 | convolution fusion | flops 3399598080 | bytes 15187968 | tf_op jit(solution)/shard_map/dot_general | solution.py:162
  403.7 13.3 %scatter_custom_fusion.1 = f32[1024,2304]{1,0:T(8,128)} fusion(s32[512]{0:T(512)S(1)} %get-tuple-element.57, f32[512,2304]{1,0:T(8,128)} %fusion.33, f32[]{:T(128)} %constant.23.clone.1), kind=kCustom, calls=%fused_computation.12 | custom fusion | flops 1179648 | bytes 9437696 | tf_op jit(solution)/shard_map/scatter-add | solution.py:168
  416.9 6.4 %convert_element_type.109 = bf16[1024,2304]{1,0:T(8,128)(2,1)} convert(f32[1024,2304]{1,0:T(8,128)} %scatter_custom_fusion.1) | non-fusion elementwise | flops 2359296 | bytes 14155776 | tf_op jit(solution)/shard_map/convert_element_type | solution.py:171
  424.1 5.7 %copy.68 = bf16[2304,720]{0,1:T(8,128)(2,1)} copy(bf16[2304,720]{1,0:T(8,128)(2,1)} %bitcast.8) | data formatting | bytes 6635520
  429.7 5.9 %copy.69 = bf16[2304,720]{0,1:T(8,128)(2,1)} copy(bf16[2304,720]{1,0:T(8,128)(2,1)} %bitcast.10) | data formatting | bytes 6635520
  435.7 5.7 %copy.70 = bf16[2304,720]{0,1:T(8,128)(2,1)} copy(bf16[2304,720]{1,0:T(8,128)(2,1)} %bitcast.12) | data formatting | bytes 6635520
  441.5 1.1 fusion.30
  442.6 2.3 copy.71
  445.1 31.4 %reduce-scatter.5.cloned.1.call-done = bf16[128,2304]{1,0:T(8,128)(2,1)} async-done(((bf16[1024,2304]{1,0:T(8,128)(2,1)}), bf16[128,2304]{1,0:T(8,128)(2,1)}) %reduce-scatter.5.cloned.1.call-update) | async-done | bytes 589840 | tf_op jit(solution)/shard_map/reduce_scatter | solution.py:170
  476.5 2.2 fusion.34
  478.8 1.0 copy.94
  (96 shorter events, 12.2 us)
Async XLA Ops:
  7.2 437.7 %copy-start = (bf16[2304,8]{0,1:T(8,128)(2,1)S(1)}, bf16[2304,8]{0,1:T(8,128)(2,1)}, u32[]{:S(2)}) copy-start(bf16[2304,8]{0,1:T(8,128)(2,1)} %param.23) | copy-start | bytes 110596
  7.2 128.3 %all-gather.4.cloned.1.call-start = ((), (), s32[]{:S(2)}) async-start(), calls=%async_computation.6 | async-start | bytes 4423680 | tf_op jit(solution)/shard_map/all_gather | solution.py:80
  35.2 6.7 %copy-start.1 = (bf16[1,128,2304]{2,1,0:T(8,128)(2,1)S(1)}, bf16[1,128,2304]{2,1,0:T(8,128)(2,1)}, u32[]{:S(2)}) copy-start(bf16[1,128,2304]{2,1,0:T(8,128)(2,1)} %param.12) | copy-start | bytes 1769476
  35.2 7.0 %copy-start.15 = (f32[2304]{0:T(1024)S(1)}, f32[2304]{0:T(1024)}, u32[]{:S(2)}) copy-start(f32[2304]{0:T(1024)} %param.21) | copy-start | bytes 27652
  41.9 120.2 %all-gather.6.cloned.1.call-start = ((), (), s32[]{:S(2)}) async-start(), calls=%async_computation.7 | async-start | bytes 1474560 | tf_op jit(solution)/shard_map/all_gather | solution.py:81
  42.4 10.3 %collective-permute-start = (bf16[128,2304]{1,0:T(8,128)(2,1)S(1)}, bf16[128,2304]{1,0:T(8,128)(2,1)S(1)}, u32[]{:S(2)}, u32[]{:S(2)}) collective-permute-start(bf16[128,2304]{1,0:T(8,128)(2,1)S(1)} %fusion.26), channel_id=1, source_target_pairs={{0,1},{1,2},{2,3},{3,4},{4,5},{5,6},{6,7},{7,0},{8,9},{9,10},{10,1... | collective-permute-start | bytes 1769480 | tf_op jit(solution)/shard_map/ppermute | solution.py:100
  52.6 10.2 %collective-permute-start.1 = (bf16[128,2304]{1,0:T(8,128)(2,1)S(1)}, bf16[128,2304]{1,0:T(8,128)(2,1)S(1)}, u32[]{:S(2)}, u32[]{:S(2)}) collective-permute-start(bf16[128,2304]{1,0:T(8,128)(2,1)S(1)} %collective-permute-done), channel_id=1, source_target_pairs={{0,1},{1,2},{2,3},{3,4},{4,5},{5,6},{6,7},{7,0},{8,9},{9,10},{10,1... | collective-permute-start | bytes 1769480 | tf_op jit(solution)/shard_map/ppermute | solution.py:100
  62.9 10.2 %collective-permute-start.2 = (bf16[128,2304]{1,0:T(8,128)(2,1)S(1)}, bf16[128,2304]{1,0:T(8,128)(2,1)S(1)}, u32[]{:S(2)}, u32[]{:S(2)}) collective-permute-start(bf16[128,2304]{1,0:T(8,128)(2,1)S(1)} %collective-permute-done.1), channel_id=1, source_target_pairs={{0,1},{1,2},{2,3},{3,4},{4,5},{5,6},{6,7},{7,0},{8,9},{9,10},{10,1... | collective-permute-start | bytes 1769480 | tf_op jit(solution)/shard_map/ppermute | solution.py:100
  73.1 10.2 %collective-permute-start.3 = (bf16[128,2304]{1,0:T(8,128)(2,1)S(1)}, bf16[128,2304]{1,0:T(8,128)(2,1)S(1)}, u32[]{:S(2)}, u32[]{:S(2)}) collective-permute-start(bf16[128,2304]{1,0:T(8,128)(2,1)S(1)} %collective-permute-done.2), channel_id=1, source_target_pairs={{0,1},{1,2},{2,3},{3,4},{4,5},{5,6},{6,7},{7,0},{8,9},{9,10},{10,1... | collective-permute-start | bytes 1769480 | tf_op jit(solution)/shard_map/ppermute | solution.py:100
  83.3 10.3 %collective-permute-start.4 = (bf16[128,2304]{1,0:T(8,128)(2,1)S(1)}, bf16[128,2304]{1,0:T(8,128)(2,1)}, u32[]{:S(2)}, u32[]{:S(2)}) collective-permute-start(bf16[128,2304]{1,0:T(8,128)(2,1)S(1)} %collective-permute-done.3), channel_id=1, source_target_pairs={{0,1},{1,2},{2,3},{3,4},{4,5},{5,6},{6,7},{7,0},{8,9},{9,10},{10,1... | collective-permute-start | bytes 1769480 | tf_op jit(solution)/shard_map/ppermute | solution.py:100
  93.6 10.5 %collective-permute-start.5 = (bf16[128,2304]{1,0:T(8,128)(2,1)}, bf16[128,2304]{1,0:T(8,128)(2,1)}, u32[]{:S(2)}, u32[]{:S(2)}) collective-permute-start(bf16[128,2304]{1,0:T(8,128)(2,1)} %collective-permute-done.4), channel_id=1, source_target_pairs={{0,1},{1,2},{2,3},{3,4},{4,5},{5,6},{6,7},{7,0},{8,9},{9,10},{10,1... | collective-permute-start | bytes 1769480 | tf_op jit(solution)/shard_map/ppermute | solution.py:100
  95.4 125.3 %reduce-scatter.3.cloned.1.call-start = ((), (), s32[]{:S(2)}) async-start(), calls=%async_computation.8 | async-start | bytes 5308416 | tf_op jit(solution)/shard_map/reduce_scatter | solution.py:127
  104.1 10.8 %collective-permute-start.6 = (bf16[128,2304]{1,0:T(8,128)(2,1)}, bf16[128,2304]{1,0:T(8,128)(2,1)}, u32[]{:S(2)}, u32[]{:S(2)}) collective-permute-start(bf16[128,2304]{1,0:T(8,128)(2,1)} %collective-permute-done.5), channel_id=1, source_target_pairs={{0,1},{1,2},{2,3},{3,4},{4,5},{5,6},{6,7},{7,0},{8,9},{9,10},{10,1... | collective-permute-start | bytes 1769480 | tf_op jit(solution)/shard_map/ppermute | solution.py:100
  137.9 7.1 %copy-start.5 = (bf16[8,4,72,3,256]{4,2,1,0,3:T(8,128)(2,1)}, bf16[8,4,72,3,256]{4,2,1,0,3:T(8,128)(2,1)S(1)}, u32[]{:S(2)}) copy-start(bf16[8,4,72,3,256]{4,2,1,0,3:T(8,128)(2,1)S(1)} %copy.62) | copy-start | bytes 10616836
  145.0 0.9 copy-start.11
  145.0 1.0 copy-start.12
  145.8 1.0 copy-start.13
  146.4 4.1 copy-start.6
  146.4 4.1 copy-start.8
  146.8 3.7 copy-start.10
  150.5 5.4 %copy-start.14 = (bf16[512,1,256]{0,2,1:T(8,128)(2,1)S(1)}, bf16[512,1,256]{0,2,1:T(8,128)(2,1)}, u32[]{:S(2)}) copy-start(bf16[512,1,256]{0,2,1:T(8,128)(2,1)} %slice.93) | copy-start | bytes 786436
  155.9 4.6 copy-start.18
  166.9 55.2 %copy-start.16 = (f32[2304]{0:T(1024)S(1)}, f32[2304]{0:T(1024)}, u32[]{:S(2)}) copy-start(f32[2304]{0:T(1024)} %param.22) | copy-start | bytes 27652
  167.0 189.9 %all-gather.8.cloned.1.call-start = ((), (), s32[]{:S(2)}) async-start(), calls=%async_computation.9 | async-start | bytes 5308416 | tf_op jit(solution)/shard_map/all_gather | solution.py:148
  242.3 58.2 %all-to-all-start.1 = ((bf16[288,8,720]{2,0,1:T(8,128)(2,1)}), bf16[288,8,720]{2,0,1:T(8,128)(2,1)}, u32[]{:S(2)}, u32[]{:S(2)}) async-start(bf16[288,8,720]{2,0,1:T(8,128)(2,1)} %copy.63), calls=%async_computation.1 | async-start | bytes 7077888 | tf_op jit(solution)/shard_map/all_to_all | solution.py:65
  300.5 46.6 %all-to-all-start.2 = ((bf16[288,8,720]{2,0,1:T(8,128)(2,1)}), bf16[288,8,720]{2,0,1:T(8,128)(2,1)}, u32[]{:S(2)}, u32[]{:S(2)}) async-start(bf16[288,8,720]{2,0,1:T(8,128)(2,1)} %copy.64), calls=%async_computation.2 | async-start | bytes 7077888 | tf_op jit(solution)/shard_map/all_to_all | solution.py:68
  323.0 28.7 %copy-start.17 = (s32[1,1024,2]{1,2,0:T(2,128)S(1)}, s32[1,1024,2]{1,2,0:T(2,128)}, u32[]{:S(2)}) copy-start(s32[1,1024,2]{1,2,0:T(2,128)} %param.15) | copy-start | bytes 24580
  347.1 46.6 %all-to-all-start.3 = ((bf16[288,8,720]{2,0,1:T(8,128)(2,1)}), bf16[288,8,720]{2,0,1:T(8,128)(2,1)}, u32[]{:S(2)}, u32[]{:S(2)}) async-start(bf16[288,8,720]{2,0,1:T(8,128)(2,1)} %copy.65), calls=%async_computation.3 | async-start | bytes 7077888 | tf_op jit(solution)/shard_map/all_to_all | solution.py:71
  351.6 124.9 %reduce-scatter.5.cloned.1.call-start = ((), (), s32[]{:S(2)}) async-start(), calls=%async_computation.10 | async-start | bytes 5308416 | tf_op jit(solution)/shard_map/reduce_scatter | solution.py:170
  435.7 5.7 %copy-start.7 = (bf16[1024,4,32]{0,2,1:T(8,128)(2,1)S(1)}, bf16[1024,4,32]{0,2,1:T(8,128)(2,1)}, u32[]{:S(2)}) copy-start(bf16[1024,4,32]{0,2,1:T(8,128)(2,1)} %copy-done.6) | copy-start | bytes 786436
  435.7 5.7 %copy-start.9 = (bf16[1024,4,32]{0,2,1:T(8,128)(2,1)S(1)}, bf16[1024,4,32]{0,2,1:T(8,128)(2,1)}, u32[]{:S(2)}) copy-start(bf16[1024,4,32]{0,2,1:T(8,128)(2,1)} %copy-done.8) | copy-start | bytes 786436
  441.4 3.4 copy-start.2
  441.4 35.1 %copy-start.3 = (bf16[128,2304]{1,0:T(8,128)(2,1)S(1)}, bf16[128,2304]{1,0:T(8,128)(2,1)}, u32[]{:S(2)}) copy-start(bf16[128,2304]{1,0:T(8,128)(2,1)} %reduce-scatter.3.cloned.1.call-done) | copy-start | bytes 1769476
  441.5 37.3 %copy-start.4 = (bf16[256,2304]{1,0:T(8,128)(2,1)S(1)}, bf16[256,2304]{1,0:T(8,128)(2,1)}, u32[]{:S(2)}) copy-start(bf16[256,2304]{1,0:T(8,128)(2,1)} %all-gather.6.cloned.1.call-done) | copy-start | bytes 3538948
Sparse Core Ops, SparseCore 0:
  42.0 69.6 all-gather.3
  113.9 29.0 all-gather.5
  167.1 53.6 reduce-scatter.2
  224.4 60.3 all-gather.7
  423.5 53.0 reduce-scatter.4
